TPU v7x, 32 devices: a whole 2x2x4 slice. The times are simulated.
32 devices in a mesh: groups: 2 (over y), ctx: 16 (over z, x, core), dp: 1.
Axes of the slice: x: 2, y: 2, z: 4, core: 2. Of those that a mesh axis runs over, the one named last changes fastest.
Arguments:
- tokens: bfloat16 [4096, 1024], P(('groups', 'ctx', 'dp')), parts along dimension 0, may hold values from -6 to 6
- cotangent: bfloat16 [4096, 1024], P(('groups', 'ctx', 'dp')), parts along dimension 0, may hold values from -6 to 6
- expert_ids: int32 [4096, 8], P(('groups', 'ctx', 'dp')), parts along dimension 0, may hold values from 0 to 15, all different within a row; in each aligned block of 128 rows (0 to 127, 128 to 255, ...) at most 80 rows name the same one
- router_weights: float32 [4096, 8], P(('groups', 'ctx', 'dp')), parts along dimension 0, may hold values from 0.03 to 0.3
- seq_lengths: int32 [8], P('groups'), parts along dimension 0, may hold values from 256 to 768, as said below
- w_gate: bfloat16 [16, 1024, 384], P('ctx', 'dp'), may hold values from -0.1875 to 0.1875
- w_up: bfloat16 [16, 1024, 384], P('ctx', 'dp'), may hold values from -0.1875 to 0.1875
- w_down: bfloat16 [16, 384, 1024], P('ctx', None, 'dp'), may hold values from -0.3125 to 0.3125
Outputs:
- mixed: bfloat16 [4096, 1024], P(('groups', 'ctx', 'dp')), parts along dimension 0
- token_grads: bfloat16 [4096, 1024], P(('groups', 'ctx', 'dp')), parts along dimension 0
- weight_grads: float32 [4096, 8], P(('groups', 'ctx', 'dp')), parts along dimension 0
There are 2 independent parts, one for each index of `groups`. A program takes and returns all parts, laid end to end along the dimension named above; an argument that names none is the same for every part. Nothing has to cross between parts.
Inputs may be any that keep to these rules, and one draw needn't show every extreme that they name: `expert_ids`: in each aligned block of 128 rows (the rows of one device) every expert is named by at most 80 rows, and in every draw some expert is named by exactly 80 rows of some block; the 8 entries of a row differ. `seq_lengths`: the 4 lengths sum to 2048; both ends of the range are reached in every draw.
All inputs are finite; a program needn't handle non-finite values.
Results may differ from a plain program's by a relative error of at most 0.0064.
Values may be sent and summed in bfloat16 or wider, within the bound.
No kernel may reach another device: no remote copies, remote signals or barrier semaphores. Data moves between devices by JAX's collectives and lax.ppermute only.
A program may use at most 128 MiB of HBM per device.

v0:
```python
import jax
import jax.numpy as jnp
from jax import lax
from jax.sharding import PartitionSpec as P


def loss_scale(position, seq_lengths, mean_length):
    ends = jnp.cumsum(seq_lengths)
    starts = ends - seq_lengths
    inside = (position[:, None] >= starts[None, :]) & (position[:, None] < ends[None, :])
    own_length = jnp.sum(jnp.where(inside, seq_lengths[None, :], 0), axis=1)
    return mean_length / own_length.astype(jnp.float32)


def forward_rows(slot_rows, gate_full, up_full, down_full):
    gate_pre = jnp.dot(slot_rows, gate_full, preferred_element_type=jnp.float32)
    up_value = jnp.dot(slot_rows, up_full, preferred_element_type=jnp.float32)
    activated = jax.nn.silu(gate_pre)
    hidden = (activated * up_value).astype(jnp.bfloat16)
    expert_out = jnp.dot(hidden, down_full, preferred_element_type=jnp.float32).astype(jnp.bfloat16)
    return (gate_pre, up_value, activated, expert_out)


def backward_rows(grad_rows, gate_pre, up_value, activated, gate_full, up_full, down_full):
    contract = (((1,), (1,)), ((), ()))
    hidden_grad = lax.dot_general(
        grad_rows, down_full, contract, preferred_element_type=jnp.float32
    )
    sigmoid_value = jax.nn.sigmoid(gate_pre)
    silu_slope = sigmoid_value * (1.0 + gate_pre * (1.0 - sigmoid_value))
    gate_grad = (hidden_grad * up_value * silu_slope).astype(jnp.bfloat16)
    up_grad = (hidden_grad * activated).astype(jnp.bfloat16)
    slot_grad = lax.dot_general(gate_grad, gate_full, contract, preferred_element_type=jnp.float32)
    slot_grad = slot_grad + lax.dot_general(
        up_grad, up_full, contract, preferred_element_type=jnp.float32
    )
    return slot_grad.astype(jnp.bfloat16)


def slot_ranks(flat_ids, experts):
    expert_hits = (flat_ids[:, None] == jnp.arange(experts, dtype=jnp.int32)[None, :]).astype(
        jnp.int32
    )
    assign_count = flat_ids.shape[0]
    row_iota = lax.broadcasted_iota(jnp.int32, (assign_count, assign_count), 0)
    col_iota = lax.broadcasted_iota(jnp.int32, (assign_count, assign_count), 1)
    lower_mask = (row_iota > col_iota).astype(jnp.bfloat16)
    earlier = jnp.dot(
        lower_mask, expert_hits.astype(jnp.bfloat16), preferred_element_type=jnp.float32
    )
    return jnp.sum(earlier * expert_hits.astype(jnp.float32), axis=1).astype(jnp.int32)


def per_device(tokens, cotangent, expert_ids, router_weights, seq_lengths, w_gate, w_up, w_down):
    ctx_count = lax.axis_size("ctx")
    dp_count = lax.axis_size("dp")
    row_count, top_count = expert_ids.shape
    slot_cap = max(2, min(row_count, row_count * top_count * 5 // (4 * ctx_count)))
    block_index = lax.axis_index("ctx") * dp_count + lax.axis_index("dp")
    position = block_index * row_count + jnp.arange(row_count, dtype=jnp.int32)
    loss_weight = loss_scale(position, seq_lengths, row_count * 4.0)
    out_grad = (cotangent.astype(jnp.float32) * loss_weight[:, None]).astype(jnp.bfloat16)
    flat_ids = expert_ids.reshape(-1)
    assign_count = flat_ids.shape[0]
    dest_slot = flat_ids * slot_cap + slot_ranks(flat_ids, ctx_count)
    source_row = jnp.full((ctx_count * slot_cap,), assign_count, jnp.int32)
    source_row = source_row.at[dest_slot].set(jnp.arange(assign_count, dtype=jnp.int32))
    filled = source_row < assign_count
    token_of = jnp.minimum(source_row, assign_count - 1) // top_count
    zero_value = jnp.zeros((), jnp.bfloat16)
    token_send = jnp.where(filled[:, None], tokens[token_of], zero_value).reshape(
        ctx_count, slot_cap, -1
    )
    grad_send = jnp.where(filled[:, None], out_grad[token_of], zero_value).reshape(
        ctx_count, slot_cap, -1
    )
    gate_full, up_full, down_full = (
        lax.all_gather(w_gate[0], "dp", axis=0, tiled=True),
        lax.all_gather(w_up[0], "dp", axis=0, tiled=True),
        lax.all_gather(w_down[0], "dp", axis=1, tiled=True),
    )
    token_arrived = lax.all_to_all(token_send, "ctx", split_axis=0, concat_axis=0, tiled=True)
    grad_arrived = lax.all_to_all(grad_send, "ctx", split_axis=0, concat_axis=0, tiled=True)
    source_count = token_arrived.shape[0]
    slot_count = token_arrived.shape[1]
    slot_rows = token_arrived.reshape(source_count * slot_count, -1)
    grad_rows = grad_arrived.reshape(source_count * slot_count, -1)
    gate_pre, up_value, activated, expert_out = forward_rows(
        slot_rows, gate_full, up_full, down_full
    )
    out_blocks = expert_out.reshape(source_count, slot_count, -1)
    slot_grad = backward_rows(
        grad_rows, gate_pre, up_value, activated, gate_full, up_full, down_full
    )
    out_home = lax.all_to_all(out_blocks, "ctx", split_axis=0, concat_axis=0, tiled=True)
    grad_home = lax.all_to_all(
        slot_grad.reshape(source_count, slot_count, -1),
        "ctx",
        split_axis=0,
        concat_axis=0,
        tiled=True,
    )
    out_rows = out_home.reshape(ctx_count * slot_cap, -1)[dest_slot].reshape(
        row_count, top_count, -1
    )
    grad_rows = grad_home.reshape(ctx_count * slot_cap, -1)[dest_slot].reshape(
        row_count, top_count, -1
    )
    mixed = jnp.sum(router_weights[:, :, None] * out_rows.astype(jnp.float32), axis=1).astype(
        jnp.bfloat16
    )
    token_grads = jnp.sum(
        router_weights[:, :, None] * grad_rows.astype(jnp.float32), axis=1
    ).astype(jnp.bfloat16)
    weight_grads = jnp.einsum("td,tkd->tk", out_grad, out_rows, preferred_element_type=jnp.float32)
    return (mixed, token_grads, weight_grads)


def solution(mesh):
    in_specs = (
        P(("groups", "ctx", "dp"), None),
        P(("groups", "ctx", "dp"), None),
        P(("groups", "ctx", "dp"), None),
        P(("groups", "ctx", "dp"), None),
        P("groups"),
        P("ctx", "dp", None),
        P("ctx", "dp", None),
        P("ctx", None, "dp"),
    )
    out_specs = (
        P(("groups", "ctx", "dp"), None),
        P(("groups", "ctx", "dp"), None),
        P(("groups", "ctx", "dp"), None),
    )
    return jax.shard_map(
        per_device, mesh=mesh, in_specs=in_specs, out_specs=out_specs, check_vma=False
    )
```

profile of v0, /device:TPU:11, one launch (start us, length us, event | category | flops | bytes accessed | tf_op | source)
XLA Modules:
  0.0 306.2 jit_solution(6240023815004228532)
XLA Ops:
  0.6 0.0 copy-start
  0.6 0.9 copy.17
  1.5 0.7 broadcast_multiply_fusion
  2.2 0.1 eq.15
  2.3 0.5 fusion.6
  2.8 0.1 copy.16
  2.9 0.1 mul.69
  3.0 4.3 %scatter_custom_fusion = s32[1280]{0:T(1024)S(1)} fusion(s32[1024]{0:T(1024)S(1)} %bitcast.49, s32[1024]{0:T(1024)S(1)} %iota.24, s32[]{:T(128)} %constant.15.clone.1), kind=kCustom, calls=%fused_computation.51 | custom fusion | bytes 5124 | tf_op jit(solution)/shard_map/scatter | solution.py:67
  7.4 0.8 reduce-window.8
  8.2 0.7 bitcast_subtract_fusion
  8.9 0.7 select_reduce_fusion
  9.6 1.1 multiply_convert_fusion.6
  10.7 0.0 copy-start.1
  10.7 5.1 %gather_fusion.2 = bf16[1280,1024]{1,0:T(8,128)(2,1)} fusion(bf16[128,1024]{1,0:T(8,128)(2,1)S(1)} %multiply_convert_fusion.6, s32[2048]{0:T(1024)S(1)} %pad_clamp_fusion), kind=kCustom, calls=%fused_computation.2 | custom fusion | bytes 5248000 | tf_op jit(solution)/shard_map/gather | solution.py:74
  15.8 0.0 copy-done.1
  15.8 5.1 %gather_fusion = bf16[1280,1024]{1,0:T(8,128)(2,1)} fusion(bf16[128,1024]{1,0:T(8,128)(2,1)S(1)} %copy-done.1, s32[2048]{0:T(1024)S(1)} %pad_clamp_fusion), kind=kCustom, calls=%fused_computation | custom fusion | bytes 5248000 | tf_op jit(solution)/shard_map/gather | solution.py:71
  20.9 0.1 broadcast_in_dim.48
  21.0 3.8 %broadcast_select_fusion = (bf16[16,80,1024]{2,1,0:T(8,128)(2,1)}, bf16[16,80,1024]{2,1,0:T(8,128)(2,1)S(1)}) fusion(bf16[16,80,1024]{2,1,0:T(8,128)(2,1)} %bitcast.42, pred[16,80]{1,0:T(8,128)(4,1)S(1)} %broadcast_in_dim.48, bf16[16,80,1024]{2,1,0:T(8,128)(2,1)} %bitcast.43), kind=kLoop, calls=%fused_computation.12 | loop fusion | flops 2621440 | bytes 10487040 | tf_op jit(solution)/shard_map/jit(_where)/select_n | solution.py:74
  24.8 64.9 %all_to_all.20 = bf16[16,80,1024]{2,1,0:T(8,128)(2,1)} all-to-all(bf16[16,80,1024]{2,1,0:T(8,128)(2,1)S(1)} %get-tuple-element.6), channel_id=1, replica_groups=mesh['groups'=2,'ctx'=16,'dp'=1] {'ctx'}, dimensions={0} | all-to-all | bytes 5242880 | tf_op jit(solution)/shard_map/all_to_all | solution.py:82
  89.7 5.1 %all-to-all-start.2 = ((bf16[16,80,1024]{2,1,0:T(8,128)(2,1)}), bf16[16,80,1024]{2,1,0:T(8,128)(2,1)S(1)}, u32[]{:S(2)}, u32[]{:S(2)}) async-start(bf16[16,80,1024]{2,1,0:T(8,128)(2,1)} %get-tuple-element.5), calls=%async_computation.2 | async-start | bytes 5242880 | tf_op jit(solution)/shard_map/all_to_all | solution.py:83
  94.8 0.0 copy-done
  94.8 0.0 copy-start.3
  94.8 0.0 copy-start.6
  94.8 4.7 %fusion.16 = f32[1280,384]{1,0:T(8,128)} fusion(bf16[1280,1024]{1,0:T(8,128)(2,1)} %bitcast.47, bf16[1,1024,384]{2,1,0:T(8,128)(2,1)S(1)} %copy-done), kind=kOutput, calls=%fused_computation.32 | convolution fusion | flops 1006632960 | bytes 5373952 | tf_op jit(solution)/shard_map/dot_general | solution.py:16
  99.5 0.0 copy-done.3
  99.5 0.0 copy-done.6
  99.5 2.9 fusion.13
  102.4 51.0 %all-to-all-done.2 = bf16[16,80,1024]{2,1,0:T(8,128)(2,1)S(1)} async-done(((bf16[16,80,1024]{2,1,0:T(8,128)(2,1)}), bf16[16,80,1024]{2,1,0:T(8,128)(2,1)S(1)}, u32[]{:S(2)}, u32[]{:S(2)}) %all-to-all-start.2) | async-done | bytes 2621472 | tf_op jit(solution)/shard_map/all_to_all | solution.py:83
  153.4 2.8 fusion.9
  156.3 0.0 copy-done.8
  156.3 0.0 copy-done.9
  156.3 0.0 copy-start.7
  156.3 1.8 fusion.7
  158.2 0.0 copy-done.7
  158.2 3.1 %add_convert_fusion = bf16[1280,1024]{1,0:T(8,128)(2,1)} fusion(f32[1280,1024]{1,0:T(8,128)S(1)} %fusion.7, f32[1280,384]{1,0:T(8,128)S(1)} %fusion.9, bf16[1,1024,384]{2,1,0:T(8,128)(2,1)S(1)} %copy-done.7, f32[1280,384]{1,0:T(8,128)S(1)} %copy-done.8), kind=kOutput, calls=%fused_computation.5 | convolution fusion | flops 1012203520 | bytes 12582912 | tf_op jit(solution)/shard_map/dot_general | solution.py:34
  161.3 4.8 %all-to-all-start.3 = ((bf16[16,80,1024]{2,1,0:T(8,128)(2,1)}), bf16[16,80,1024]{2,1,0:T(8,128)(2,1)S(1)}, u32[]{:S(2)}, u32[]{:S(2)}) async-start(bf16[16,80,1024]{2,1,0:T(8,128)(2,1)} %bitcast.46), calls=%async_computation.3 | async-start | bytes 5242880 | tf_op jit(solution)/shard_map/all_to_all | solution.py:96
  166.1 5.4 %convolution_convert_fusion = bf16[1280,1024]{1,0:T(8,128)(2,1)} fusion(f32[1280,384]{1,0:T(8,128)} %fusion.13, bf16[1,384,1024]{2,1,0:T(8,128)(2,1)} %param.15, f32[1280,384]{1,0:T(8,128)} %fusion.16), kind=kOutput, calls=%fused_computation.11 | convolution fusion | flops 1010892800 | bytes 7340032 | tf_op jit(solution)/shard_map/dot_general | solution.py:20
  171.4 53.3 %all-to-all-done.3 = bf16[16,80,1024]{2,1,0:T(8,128)(2,1)S(1)} async-done(((bf16[16,80,1024]{2,1,0:T(8,128)(2,1)}), bf16[16,80,1024]{2,1,0:T(8,128)(2,1)S(1)}, u32[]{:S(2)}, u32[]{:S(2)}) %all-to-all-start.3) | async-done | bytes 2621472 | tf_op jit(solution)/shard_map/all_to_all | solution.py:96
  224.7 4.9 %all-to-all-start.1 = ((bf16[16,80,1024]{2,1,0:T(8,128)(2,1)}), bf16[16,80,1024]{2,1,0:T(8,128)(2,1)}, u32[]{:S(2)}, u32[]{:S(2)}) async-start(bf16[16,80,1024]{2,1,0:T(8,128)(2,1)} %bitcast.44), calls=%async_computation.1 | async-start | bytes 5242880 | tf_op jit(solution)/shard_map/all_to_all | solution.py:95
  229.6 0.0 copy-done.5
  229.6 0.1 copy.15
  229.8 1.8 fusion.32
  231.5 5.4 %gather_fusion.3 = bf16[1024,1024]{1,0:T(8,128)(2,1)} fusion(bf16[1280,1024]{1,0:T(8,128)(2,1)S(1)} %bitcast.41, s32[1024]{0:T(1024)S(1)} %broadcast_clamp_fusion), kind=kCustom, calls=%fused_computation.3 | custom fusion | bytes 4198400 | tf_op jit(solution)/shard_map/gather | solution.py:106
  236.9 51.5 %all-to-all-done.1 = bf16[16,80,1024]{2,1,0:T(8,128)(2,1)} async-done(((bf16[16,80,1024]{2,1,0:T(8,128)(2,1)}), bf16[16,80,1024]{2,1,0:T(8,128)(2,1)}, u32[]{:S(2)}, u32[]{:S(2)}) %all-to-all-start.1) | async-done | bytes 2621472 | tf_op jit(solution)/shard_map/all_to_all | solution.py:95
  288.4 8.1 %gather_fusion.1 = bf16[1024,1024]{1,0:T(8,128)(2,1)} fusion(bf16[1280,1024]{1,0:T(8,128)(2,1)} %bitcast.8, s32[1024]{0:T(1024)S(1)} %broadcast_clamp_fusion), kind=kCustom, calls=%fused_computation.1 | custom fusion | bytes 4198400 | tf_op jit(solution)/shard_map/gather | solution.py:103
  296.5 3.0 fusion.2
  299.5 0.7 copy.19
  300.2 6.0 %fusion = (bf16[128,1024]{1,0:T(8,128)(2,1)}, bf16[128,1024]{1,0:T(8,128)(2,1)}) fusion(bf16[1024,1024]{1,0:T(8,128)(2,1)S(1)} %copy-done.2, f32[128,8]{1,0:T(8,128)S(1)} %copy.15, bf16[1024,1024]{1,0:T(8,128)(2,1)} %gather_fusion.1), kind=kLoop, calls=%fused_computation.7 | loop fusion | flops 6029312 | bytes 4722688 | tf_op jit(solution)/shard_map/reduce_sum | solution.py:112
  (16 shorter events, 0.1 us)
Async XLA Ops:
  0.6 94.2 %copy-start = (bf16[1,1024,384]{2,1,0:T(8,128)(2,1)S(1)}, bf16[1,1024,384]{2,1,0:T(8,128)(2,1)}, u32[]{:S(2)}) copy-start(bf16[1,1024,384]{2,1,0:T(8,128)(2,1)} %param.13) | copy-start | bytes 2359300
  10.7 5.1 %copy-start.1 = (bf16[128,1024]{1,0:T(8,128)(2,1)S(1)}, bf16[128,1024]{1,0:T(8,128)(2,1)}, u32[]{:S(2)}) copy-start(bf16[128,1024]{1,0:T(8,128)(2,1)} %param.8) | copy-start | bytes 786436
  89.7 63.7 %all-to-all-start.2 = ((bf16[16,80,1024]{2,1,0:T(8,128)(2,1)}), bf16[16,80,1024]{2,1,0:T(8,128)(2,1)S(1)}, u32[]{:S(2)}, u32[]{:S(2)}) async-start(bf16[16,80,1024]{2,1,0:T(8,128)(2,1)} %get-tuple-element.5), calls=%async_computation.2 | async-start | bytes 5242880 | tf_op jit(solution)/shard_map/all_to_all | solution.py:83
  94.8 4.7 %copy-start.3 = (bf16[16,80,1024]{2,1,0:T(8,128)(2,1)S(1)}, bf16[16,80,1024]{2,1,0:T(8,128)(2,1)}, u32[]{:S(2)}) copy-start(bf16[16,80,1024]{2,1,0:T(8,128)(2,1)} %all_to_all.20) | copy-start | bytes 7864324
  94.8 4.7 %copy-start.6 = (bf16[1,1024,384]{2,1,0:T(8,128)(2,1)S(1)}, bf16[1,1024,384]{2,1,0:T(8,128)(2,1)}, u32[]{:S(2)}) copy-start(bf16[1,1024,384]{2,1,0:T(8,128)(2,1)} %param.14) | copy-start | bytes 2359300
  153.4 2.9 copy-start.8
  153.4 2.9 copy-start.9
  156.3 1.8 copy-start.7
  161.3 63.4 %all-to-all-start.3 = ((bf16[16,80,1024]{2,1,0:T(8,128)(2,1)}), bf16[16,80,1024]{2,1,0:T(8,128)(2,1)S(1)}, u32[]{:S(2)}, u32[]{:S(2)}) async-start(bf16[16,80,1024]{2,1,0:T(8,128)(2,1)} %bitcast.46), calls=%async_computation.3 | async-start | bytes 5242880 | tf_op jit(solution)/shard_map/all_to_all | solution.py:96
  224.7 4.9 %copy-start.5 = (f32[128,8]{0,1:T(8,128)S(1)}, f32[128,8]{0,1:T(8,128)}, u32[]{:S(2)}) copy-start(f32[128,8]{0,1:T(8,128)} %param.11) | copy-start | bytes 12292
  224.7 63.7 %all-to-all-start.1 = ((bf16[16,80,1024]{2,1,0:T(8,128)(2,1)}), bf16[16,80,1024]{2,1,0:T(8,128)(2,1)}, u32[]{:S(2)}, u32[]{:S(2)}) async-start(bf16[16,80,1024]{2,1,0:T(8,128)(2,1)} %bitcast.44), calls=%async_computation.1 | async-start | bytes 5242880 | tf_op jit(solution)/shard_map/all_to_all | solution.py:95
  288.4 8.1 %copy-start.4 = (bf16[128,1024,1]{1,0,2:T(8,128)(2,1)S(1)}, bf16[128,1024,1]{1,0,2:T(8,128)(2,1)}, u32[]{:S(2)}) copy-start(bf16[128,1024,1]{1,0,2:T(8,128)(2,1)} %fusion.32) | copy-start | bytes 786436
  296.5 3.6 %copy-start.2 = (bf16[1024,1024]{1,0:T(8,128)(2,1)S(1)}, bf16[1024,1024]{1,0:T(8,128)(2,1)}, u32[]{:S(2)}) copy-start(bf16[1024,1024]{1,0:T(8,128)(2,1)} %gather_fusion.3) | copy-start | bytes 6291460
where the time goes:
time: 307 us; the launch traced here: 306 us
  waiting for transfers between devices  156 us (51%)
  blocking collectives  64.9 us (21%)
  local copies, waits for them, and re-layouts  30 us (10%)
  matrix products  24.2 us (8%)
  other arithmetic  15.7 us (5%)
  starting transfers between devices  14.7 us (5%)
    all_to_all x1, blocking collectives, per_device(): lax.all_to_all(token_send, 'ctx', split_axis=0, concat_axis=0, tiled=True)  64.9 us
    all_to_all x1, waiting for transfers between devices, per_device(): lax.all_to_all(slot_grad.reshape(source_count, slot_count, -1), 'ctx', sp...  53.3 us
    all_to_all x1, waiting for transfers between devices, per_device(): lax.all_to_all(out_blocks, 'ctx', split_axis=0, concat_axis=0, tiled=True)  51.5 us
    all_to_all x1, waiting for transfers between devices, per_device(): lax.all_to_all(grad_send, 'ctx', split_axis=0, concat_axis=0, tiled=True)  51 us
    gather x1, local copies, waits for them, and re-layouts, per_device(): out_home.reshape(ctx_count * slot_cap, -1)[dest_slot]  8.13 us
  transfers between devices with their start and end apart: 3, of which 3 were waited for; matrix products, arithmetic and copies ran while one was open for 7% of the time, Pallas kernels for 0%

commit v1 on v0

--- a/solution.py
+++ b/solution.py
@@ -1,7 +1,16 @@
+import functools
+
 import jax
 import jax.numpy as jnp
 from jax import lax
+from jax.experimental import pallas as pl
+from jax.experimental.pallas import tpu as pltpu
 from jax.sharding import PartitionSpec as P
+
+LANES = 128
+CHUNK = 256
+TERMS = 3
+CORE_BIT, WEIGHT_BIT, NEAR_BIT, FAR_BIT = 1, 2, 4, 8
 
 
 def loss_scale(position, seq_lengths, mean_length):
@@ -51,7 +60,7 @@
     return jnp.sum(earlier * expert_hits.astype(jnp.float32), axis=1).astype(jnp.int32)
 
 
-def per_device(tokens, cotangent, expert_ids, router_weights, seq_lengths, w_gate, w_up, w_down):
+def per_device_sparse(tokens, cotangent, expert_ids, router_weights, seq_lengths, w_gate, w_up, w_down):
     ctx_count = lax.axis_size("ctx")
     dp_count = lax.axis_size("dp")
     row_count, top_count = expert_ids.shape
@@ -116,6 +125,354 @@
     return (mixed, token_grads, weight_grads)
 
 
+def prep_kernel(mean_length, experts, base_ref, seq_ref, tok_ref, cot_ref, ids_ref, rw_ref, tp_ref, grad_ref):
+    rows, width = tok_ref.shape
+    position = base_ref[0] + lax.broadcasted_iota(jnp.int32, (rows, 1), 0)
+    own_length = jnp.zeros((rows, 1), jnp.int32)
+    start = jnp.int32(0)
+    for s in range(seq_ref.shape[0]):
+        length = seq_ref[s]
+        inside = (position >= start) & (position < start + length)
+        own_length = jnp.where(inside, length, own_length)
+        start = start + length
+    loss_weight = mean_length / own_length.astype(jnp.float32)
+    grad_ref[...] = (cot_ref[...].astype(jnp.float32) * loss_weight).astype(jnp.bfloat16)
+    lane = lax.broadcasted_iota(jnp.int32, (rows, LANES), 1)
+    expert = lax.rem(lane, experts)
+    dense = jnp.zeros((rows, LANES), jnp.float32)
+    for k in range(ids_ref.shape[1]):
+        dense = dense + jnp.where(ids_ref[:, k : k + 1] == expert, rw_ref[:, k : k + 1], 0.0)
+    high = dense.astype(jnp.bfloat16).astype(jnp.float32)
+    middle = (dense - high).astype(jnp.bfloat16).astype(jnp.float32)
+    low = dense - high - middle
+    packed = jnp.where(lane < experts, high, jnp.where(lane < 2 * experts, middle, low))
+    packed = jnp.where(lane < TERMS * experts, packed, 0.0)
+    tp_ref[:, :width] = tok_ref[...]
+    tp_ref[:, width:] = packed.astype(jnp.bfloat16)
+
+
+def route_columns(packed, experts, expert_of):
+    lane = lax.broadcasted_iota(jnp.int32, packed.shape, 1)
+    own = lax.rem(lane, experts)
+    wide = packed.astype(jnp.float32)
+    return [
+        jnp.sum(jnp.where(own == e, wide, 0.0), axis=1, keepdims=True) for e in expert_of
+    ]
+
+
+def start_all(copies):
+    for c in copies:
+        c.start()
+
+
+def forward_kernel(experts, count, which_ref, *refs):
+    tokens, gates, ups, downs = refs[:4], refs[4 : 4 + count], refs[4 + count : 4 + 2 * count], refs[4 + 2 * count : 4 + 3 * count]
+    keep_ref, send_ref, act_ref, slope_ref, hid_ref = refs[4 + 3 * count : 9 + 3 * count]
+    x_ref, g_ref, u_ref, d_ref, hw_ref, sem = refs[9 + 3 * count :]
+    rows = tokens[0].shape[0]
+    width, ff = gates[0].shape
+    t_copies = [
+        pltpu.make_async_copy(t, x_ref.at[pl.ds(i * rows, rows)], sem.at[i]) for i, t in enumerate(tokens)
+    ]
+    w_copies = []
+    for e in range(count):
+        cols = pl.ds(e * ff, ff)
+        w_copies.append((
+            pltpu.make_async_copy(gates[e], g_ref.at[:, cols], sem.at[4 + 3 * e]),
+            pltpu.make_async_copy(ups[e], u_ref.at[:, cols], sem.at[5 + 3 * e]),
+            pltpu.make_async_copy(downs[e], d_ref.at[cols, :], sem.at[6 + 3 * e]),
+        ))
+    start_all(t_copies)
+    for e in range(count):
+        start_all(w_copies[e][:2])
+    for e in range(count):
+        w_copies[e][2].start()
+    for c in t_copies:
+        c.wait()
+    scale = route_columns(x_ref[:, width:], experts, [which_ref[e] for e in range(count)])
+    x = x_ref[:, :width]
+    ready = 0
+    for lo in range(0, count * ff, CHUNK):
+        while ready < count and ready * ff < lo + CHUNK:
+            w_copies[ready][0].wait()
+            w_copies[ready][1].wait()
+            ready += 1
+        gate = jnp.dot(x, g_ref[:, lo : lo + CHUNK], preferred_element_type=jnp.float32)
+        up = jnp.dot(x, u_ref[:, lo : lo + CHUNK], preferred_element_type=jnp.float32)
+        for j in range(0, CHUNK, LANES):
+            cols = slice(lo + j, lo + j + LANES)
+            g = gate[:, j : j + LANES]
+            u = up[:, j : j + LANES]
+            sigmoid = 1.0 / (1.0 + jnp.exp(-g))
+            act = g * sigmoid
+            hidden = act * u
+            act_ref[:, cols] = act.astype(jnp.bfloat16)
+            slope_ref[:, cols] = (u * (sigmoid * (1.0 + g * (1.0 - sigmoid)))).astype(jnp.bfloat16)
+            hid_ref[:, cols] = hidden.astype(jnp.bfloat16)
+            hw_ref[:, cols] = (hidden * scale[(lo + j) // ff]).astype(jnp.bfloat16)
+    for e in range(count):
+        w_copies[e][2].wait()
+    hw = hw_ref[...]
+    for lo in range(0, width, CHUNK):
+        cols = slice(lo, lo + CHUNK)
+        out = jnp.dot(hw, d_ref[:, cols], preferred_element_type=jnp.float32)
+        keep_ref[0, :, cols] = out[:rows]
+        send_ref[0, :, cols] = out[rows : 2 * rows].astype(jnp.bfloat16)
+        keep_ref[1, :, cols] = out[2 * rows : 3 * rows]
+        send_ref[1, :, cols] = out[3 * rows :].astype(jnp.bfloat16)
+
+
+def backward_kernel(experts, count, which_ref, *refs):
+    grads, gates, ups, downs = refs[:4], refs[4 : 4 + count], refs[4 + count : 4 + 2 * count], refs[4 + 2 * count : 4 + 3 * count]
+    routes = refs[4 + 3 * count : 8 + 3 * count]
+    act_ref, slope_ref, hid_ref = refs[8 + 3 * count : 11 + 3 * count]
+    keep_ref, send_ref = refs[11 + 3 * count : 13 + 3 * count]
+    x_ref, g_ref, u_ref, d_ref, r_ref, gg_ref, ug_ref, sem = refs[13 + 3 * count :]
+    rows = grads[0].shape[0]
+    width, ff = gates[0].shape
+    t_copies = [
+        pltpu.make_async_copy(t, x_ref.at[pl.ds(i * rows, rows)], sem.at[i]) for i, t in enumerate(grads)
+    ] + [
+        pltpu.make_async_copy(t.at[:, pl.ds(width, LANES)], r_ref.at[pl.ds(i * rows, rows)], sem.at[4 + 3 * count + i])
+        for i, t in enumerate(routes)
+    ]
+    w_copies = []
+    for e in range(count):
+        cols = pl.ds(e * ff, ff)
+        w_copies.append((
+            pltpu.make_async_copy(gates[e], g_ref.at[:, cols], sem.at[4 + 3 * e]),
+            pltpu.make_async_copy(ups[e], u_ref.at[:, cols], sem.at[5 + 3 * e]),
+            pltpu.make_async_copy(downs[e], d_ref.at[cols, :], sem.at[6 + 3 * e]),
+        ))
+    start_all(t_copies)
+    for e in range(count):
+        w_copies[e][2].start()
+    for e in range(count):
+        start_all(w_copies[e][:2])
+    for c in t_copies:
+        c.wait()
+    scale = route_columns(r_ref[...], experts, [which_ref[e] for e in range(count)])
+    x = x_ref[...]
+    contract = (((1,), (1,)), ((), ()))
+    inner = [jnp.zeros((4 * rows, LANES), jnp.float32) for _ in range(count)]
+    ready = 0
+    for lo in range(0, count * ff, CHUNK):
+        while ready < count and ready * ff < lo + CHUNK:
+            w_copies[ready][2].wait()
+            ready += 1
+        hidden_grad = lax.dot_general(x, d_ref[lo : lo + CHUNK, :], contract, preferred_element_type=jnp.float32)
+        for j in range(0, CHUNK, LANES):
+            cols = slice(lo + j, lo + j + LANES)
+            e = (lo + j) // ff
+            hg = hidden_grad[:, j : j + LANES]
+            inner[e] = inner[e] + hg * hid_ref[:, cols].astype(jnp.float32)
+            weighted = hg * scale[e]
+            gg_ref[:, cols] = (weighted * slope_ref[:, cols].astype(jnp.float32)).astype(jnp.bfloat16)
+            ug_ref[:, cols] = (weighted * act_ref[:, cols].astype(jnp.float32)).astype(jnp.bfloat16)
+    lane = lax.broadcasted_iota(jnp.int32, (4 * rows, LANES), 1)
+    table = jnp.zeros((4 * rows, LANES), jnp.float32)
+    own = lax.rem(lane, experts)
+    for e in range(count):
+        total = jnp.sum(inner[e], axis=1, keepdims=True)
+        table = table + jnp.where(own == which_ref[e], total, 0.0)
+    high = table.astype(jnp.bfloat16).astype(jnp.float32)
+    middle = (table - high).astype(jnp.bfloat16).astype(jnp.float32)
+    low = table - high - middle
+    packed = jnp.where(lane < experts, high, jnp.where(lane < 2 * experts, middle, low))
+    packed = jnp.where(lane < TERMS * experts, packed, 0.0)
+
+    def put(cols, out):
+        keep_ref[0, :, cols] = out[:rows]
+        send_ref[0, :, cols] = out[rows : 2 * rows].astype(jnp.bfloat16)
+        keep_ref[1, :, cols] = out[2 * rows : 3 * rows]
+        send_ref[1, :, cols] = out[3 * rows :].astype(jnp.bfloat16)
+
+    put(slice(width, width + LANES), packed)
+    for e in range(count):
+        w_copies[e][0].wait()
+        w_copies[e][1].wait()
+    gg = gg_ref[...]
+    ug = ug_ref[...]
+    for lo in range(0, width, CHUNK):
+        out = lax.dot_general(gg, g_ref[lo : lo + CHUNK, :], contract, preferred_element_type=jnp.float32)
+        out = out + lax.dot_general(ug, u_ref[lo : lo + CHUNK, :], contract, preferred_element_type=jnp.float32)
+        put(slice(lo, lo + CHUNK), out)
+
+
+def merge_kernel(keep_ref, got_ref, out_ref):
+    out_ref[...] = (keep_ref[0] + got_ref[0].astype(jnp.float32)).astype(jnp.bfloat16)
+
+
+def finish_mixed_kernel(keep_ref, near_ref, far_ref, out_ref):
+    total = keep_ref[0] + near_ref[0].astype(jnp.float32) + far_ref[...].astype(jnp.float32)
+    out_ref[...] = total.astype(jnp.bfloat16)
+
+
+def finish_grad_kernel(experts, keep_ref, near_ref, far_ref, ids_ref, out_ref, wg_ref):
+    total = keep_ref[0] + near_ref[0].astype(jnp.float32) + far_ref[...].astype(jnp.float32)
+    width = out_ref.shape[1]
+    out_ref[...] = total[:, :width].astype(jnp.bfloat16)
+    table = total[:, width:]
+    own = lax.rem(lax.broadcasted_iota(jnp.int32, table.shape, 1), experts)
+    picked = [
+        jnp.sum(jnp.where(own == ids_ref[:, k : k + 1], table, 0.0), axis=1, keepdims=True)
+        for k in range(ids_ref.shape[1])
+    ]
+    wg_ref[...] = jnp.concatenate(picked, axis=1)
+
+
+def whole(count=1):
+    return [pl.BlockSpec(memory_space=pltpu.VMEM)] * count
+
+
+def in_place(count=1):
+    return [pl.BlockSpec(memory_space=pl.ANY)] * count
+
+
+def scalars(count=1):
+    return [pl.BlockSpec(memory_space=pltpu.SMEM)] * count
+
+
+def per_device_dense(tokens, cotangent, expert_ids, router_weights, seq_lengths, w_gate, w_up, w_down):
+    experts = lax.axis_size("ctx")
+    rows, width = tokens.shape
+    ff = w_gate.shape[2]
+    me = lax.axis_index("ctx")
+    bf16, f32 = jnp.bfloat16, jnp.float32
+    shape = jax.ShapeDtypeStruct
+
+    def swap(value, bit):
+        return lax.ppermute(value, "ctx", [(i, i ^ bit) for i in range(experts)])
+
+    base = (me * rows).astype(jnp.int32).reshape(1)
+    mine, grad = pl.pallas_call(
+        functools.partial(prep_kernel, rows * 4.0, experts),
+        in_specs=scalars(2) + whole(4),
+        out_specs=whole(2),
+        out_shape=[shape((rows, width + LANES), bf16), shape((rows, width), bf16)],
+        name="prep",
+    )(base, seq_lengths, tokens, cotangent, expert_ids, router_weights)
+
+    far = swap(mine, FAR_BIT)
+    near = swap(mine, NEAR_BIT)
+    both = swap(far, NEAR_BIT)
+    token_blocks = [mine, near, far, both]
+    weights = [w_gate[0], w_up[0], w_down[0]]
+    gathered = []
+    for w in weights:
+        core = swap(w, CORE_BIT)
+        other = swap(w, WEIGHT_BIT)
+        other_core = swap(other, CORE_BIT)
+        gathered.append([w, core, other, other_core])
+    count = 4
+    which = jnp.stack([me, me ^ CORE_BIT, me ^ WEIGHT_BIT, me ^ (CORE_BIT | WEIGHT_BIT)]).astype(jnp.int32)
+    g_far = swap(grad, FAR_BIT)
+    g_near = swap(grad, NEAR_BIT)
+    g_both = swap(g_far, NEAR_BIT)
+    grad_blocks = [grad, g_near, g_far, g_both]
+    inner = count * ff
+    all_rows = 4 * rows
+    weight_scratch = [
+        pltpu.VMEM((width, inner), bf16),
+        pltpu.VMEM((width, inner), bf16),
+        pltpu.VMEM((inner, width), bf16),
+    ]
+    flops = 2 * all_rows * width * inner * 3
+    keep, send, act, slope, hid = pl.pallas_call(
+        functools.partial(forward_kernel, experts, count),
+        in_specs=scalars(1) + in_place(4 + 3 * count),
+        out_specs=whole(5),
+        out_shape=[
+            shape((2, rows, width), f32),
+            shape((2, rows, width), bf16),
+            shape((all_rows, inner), bf16),
+            shape((all_rows, inner), bf16),
+            shape((all_rows, inner), bf16),
+        ],
+        scratch_shapes=[pltpu.VMEM((all_rows, width + LANES), bf16)] + weight_scratch
+        + [pltpu.VMEM((all_rows, inner), bf16), pltpu.SemaphoreType.DMA((4 + 3 * count,))],
+        cost_estimate=pl.CostEstimate(flops=flops, bytes_accessed=6 * width * inner + 6 * all_rows * inner, transcendentals=all_rows * inner),
+        name="forward",
+    )(which, *token_blocks, *gathered[0], *gathered[1], *gathered[2])
+
+    def gather_back(keep, send, tag):
+        wide = send.shape[2]
+        got = swap(send, NEAR_BIT)
+        outgoing = pl.pallas_call(
+            merge_kernel,
+            grid=(1,),
+            in_specs=[
+                pl.BlockSpec((1, rows, wide), lambda i: (1, 0, 0)),
+                pl.BlockSpec((1, rows, wide), lambda i: (1, 0, 0)),
+            ],
+            out_specs=pl.BlockSpec((rows, wide), lambda i: (0, 0)),
+            out_shape=shape((rows, wide), bf16),
+            name="merge_" + tag,
+        )(keep, got)
+        return got, swap(outgoing, FAR_BIT)
+
+    got, came = gather_back(keep, send, "mixed")
+    g_keep, g_send = pl.pallas_call(
+        functools.partial(backward_kernel, experts, count),
+        in_specs=scalars(1) + in_place(8 + 3 * count) + whole(3),
+        out_specs=whole(2),
+        out_shape=[shape((2, rows, width + LANES), f32), shape((2, rows, width + LANES), bf16)],
+        scratch_shapes=[pltpu.VMEM((all_rows, width), bf16)] + weight_scratch
+        + [
+            pltpu.VMEM((all_rows, LANES), bf16),
+            pltpu.VMEM((all_rows, inner), bf16),
+            pltpu.VMEM((all_rows, inner), bf16),
+            pltpu.SemaphoreType.DMA((8 + 3 * count,)),
+        ],
+        cost_estimate=pl.CostEstimate(flops=flops, bytes_accessed=6 * width * inner + 6 * all_rows * inner, transcendentals=0),
+        name="backward",
+    )(which, *grad_blocks, *gathered[0], *gathered[1], *gathered[2], *token_blocks, act, slope, hid)
+    g_got, g_came = gather_back(g_keep, g_send, "grad")
+
+    def first(wide):
+        return pl.BlockSpec((1, rows, wide), lambda i: (0, 0, 0))
+
+    def flat(wide):
+        return pl.BlockSpec((rows, wide), lambda i: (0, 0))
+
+    mixed = pl.pallas_call(
+        finish_mixed_kernel,
+        grid=(1,),
+        in_specs=[first(width), first(width), flat(width)],
+        out_specs=flat(width),
+        out_shape=shape((rows, width), bf16),
+        name="finish_mixed",
+    )(keep, got, came)
+    top = expert_ids.shape[1]
+    token_grads, weight_grads = pl.pallas_call(
+        functools.partial(finish_grad_kernel, experts),
+        grid=(1,),
+        in_specs=[first(width + LANES), first(width + LANES), flat(width + LANES), flat(top)],
+        out_specs=[flat(width), flat(top)],
+        out_shape=[shape((rows, width), bf16), shape((rows, top), f32)],
+        name="finish_grad",
+    )(g_keep, g_got, g_came, expert_ids)
+    return mixed, token_grads, weight_grads
+
+
+def spread_fits(mesh, args):
+    tokens, expert_ids, w_gate = args[0], args[2], args[5]
+    ctx = mesh.shape["ctx"]
+    ff = w_gate.shape[2]
+    block = tokens.shape[0] // (mesh.shape["groups"] * ctx * mesh.shape["dp"])
+    return (
+        mesh.shape["dp"] == 1
+        and w_gate.shape[0] == ctx
+        and ctx == 2 * FAR_BIT
+        and expert_ids.shape[1] * 2 >= ctx
+        and TERMS * ctx <= LANES
+        and tokens.shape[1] % CHUNK == 0
+        and ff % LANES == 0
+        and (4 * ff) % CHUNK == 0
+        and block % 16 == 0
+    )
+
+
 def solution(mesh):
     in_specs = (
         P(("groups", "ctx", "dp"), None),
@@ -132,6 +489,11 @@
         P(("groups", "ctx", "dp"), None),
         P(("groups", "ctx", "dp"), None),
     )
-    return jax.shard_map(
-        per_device, mesh=mesh, in_specs=in_specs, out_specs=out_specs, check_vma=False
-    )
+
+    def step(*args):
+        per_device = per_device_dense if spread_fits(mesh, args) else per_device_sparse
+        return jax.shard_map(
+            per_device, mesh=mesh, in_specs=in_specs, out_specs=out_specs, check_vma=False
+        )(*args)
+
+    return step

time: 307 us -> 148 us (0.48)
  the two profiles are of different devices: /device:TPU:11 before, /device:TPU:0 now
where the time goes in v1:
time: 148 us
  waiting for transfers between devices  89.4 us (60%)
  Pallas kernels  34.2 us (23%)
  starting transfers between devices  15.1 us (10%)
  local copies, waits for them, and re-layouts  7.4 us (5%)
    ppermute x19, waiting for transfers between devices, swap(): return lax.ppermute(value, 'ctx', [(i, i ^ bit) for i in range(experts)])  89.4 us
    ppermute x19, starting transfers between devices, swap(): return lax.ppermute(value, 'ctx', [(i, i ^ bit) for i in range(experts)])  15.1 us
    pallas_call x1, Pallas kernels, per_device_dense(): pl.pallas_call(functools.partial(backward_kernel, experts, count), in_spe...  12.4 us
    pallas_call x1, Pallas kernels, per_device_dense(): pl.pallas_call(functools.partial(forward_kernel, experts, count), in_spec...  11 us
    unnamed x29, local copies, waits for them, and re-layouts  7.4 us
    pallas_call x2, Pallas kernels, gather_back(): pl.pallas_call(merge_kernel, grid=(1,), in_specs=[pl.BlockSpec((1, rows,...  3.75 us
  transfers between devices with their start and end apart: 19, of which 9 were waited for; matrix products, arithmetic and copies ran while one was open for 1% of the time, Pallas kernels for 11%

profile of v1, /device:TPU:0, one launch (start us, length us, event | category | flops | bytes accessed | tf_op | source)
XLA Modules:
  0.0 147.5 jit_solution(10929446306263506075)
XLA Ops:
  0.6 1.4 copy.11.ids_ref
  2.0 1.4 copy.12.rw_ref
  3.5 2.3 %prep.1 = (bf16[128,1152]{1,0:T(8,128)(2,1)}, bf16[128,1024]{1,0:T(8,128)(2,1)}) custom-call(s32[1]{0:T(128)} %bitcast.4.base_ref, s32[4]{0:T(128)} %seq_ref.1, bf16[128,1024]{1,0:T(8,128)(2,1)} %tok_ref.1, bf16[128,1024]{1,0:T(8,128)(2,1)} %cot_ref.1, s32[128,8]{1,0:T(8,128)} %copy.11.ids_ref, f32[128,8]{1,0:T(8,128)} %copy.12.rw_ref), custom_call_target="tpu_custom_call" | custom-call | tf_op jit(solution)/shard_map/prep/pallas_call | solution.py:348
  5.7 4.1 %collective-permute-start.15 = (bf16[128,1024]{1,0:T(8,128)(2,1)}, bf16[128,1024]{1,0:T(8,128)(2,1)S(1)}, u32[]{:S(2)}, u32[]{:S(2)}) collective-permute-start(bf16[128,1024]{1,0:T(8,128)(2,1)} %get-tuple-element.17.refs_0_), channel_id=1, source_target_pairs={{0,8},{1,9},{2,10},{3,11},{4,12},{5,13},{6,14},{7,15},{8,0},{9,1},... | collective-permute-start | bytes 786440 | tf_op jit(solution)/shard_map/ppermute | solution.py:345
  9.8 1.6 %collective-permute-start = (bf16[128,1152]{1,0:T(8,128)(2,1)}, bf16[128,1152]{1,0:T(8,128)(2,1)S(1)}, u32[]{:S(2)}, u32[]{:S(2)}) collective-permute-start(bf16[128,1152]{1,0:T(8,128)(2,1)} %get-tuple-element.14.refs_0_.refs_16_), channel_id=1, source_target_pairs={{0,4},{1,5},{2,6},{3,7},{4,0},{5,1},{6,2},{7,3},{8,12},{9,13},{10,... | collective-permute-start | bytes 884744 | tf_op jit(solution)/shard_map/ppermute | solution.py:345
  11.4 0.0 collective-permute-start.3
  11.4 1.5 %collective-permute-start.4 = (bf16[1024,384]{1,0:T(8,128)(2,1)}, bf16[1024,384]{1,0:T(8,128)(2,1)S(1)}, u32[]{:S(2)}, u32[]{:S(2)}) collective-permute-start(bf16[1024,384]{1,0:T(8,128)(2,1)} %bitcast.9), channel_id=1, source_target_pairs={{0,2},{1,3},{2,0},{3,1},{4,6},{5,7},{6,4},{7,5},{8,10},{9,11},{10,... | collective-permute-start | bytes 2359304 | tf_op jit(solution)/shard_map/ppermute | solution.py:345
  12.9 0.5 collective-permute-start.7
  13.4 8.6 %collective-permute-done.15.refs_2_ = bf16[128,1024]{1,0:T(8,128)(2,1)S(1)} collective-permute-done((bf16[128,1024]{1,0:T(8,128)(2,1)}, bf16[128,1024]{1,0:T(8,128)(2,1)S(1)}, u32[]{:S(2)}, u32[]{:S(2)}) %collective-permute-start.15) | collective-permute-done | bytes 262176 | tf_op jit(solution)/shard_map/ppermute | solution.py:345
  22.0 1.5 %collective-permute-start.10 = (bf16[384,1024]{1,0:T(8,128)(2,1)}, bf16[384,1024]{1,0:T(8,128)(2,1)S(1)}, u32[]{:S(2)}, u32[]{:S(2)}) collective-permute-start(bf16[384,1024]{1,0:T(8,128)(2,1)} %bitcast.16), channel_id=1, source_target_pairs={{0,2},{1,3},{2,0},{3,1},{4,6},{5,7},{6,4},{7,5},{8,10},{9,11},{10,... | collective-permute-start | bytes 2359304 | tf_op jit(solution)/shard_map/ppermute | solution.py:345
  23.6 0.0 collective-permute-done.refs_1_.refs_17_
  23.6 0.7 collective-permute-start.1
  24.3 14.3 %collective-permute-done.1.refs_2_.refs_18_ = bf16[128,1152]{1,0:T(8,128)(2,1)S(1)} collective-permute-done((bf16[128,1152]{1,0:T(8,128)(2,1)}, bf16[128,1152]{1,0:T(8,128)(2,1)S(1)}, u32[]{:S(2)}, u32[]{:S(2)}) %collective-permute-start.1) | collective-permute-done | bytes 294944 | tf_op jit(solution)/shard_map/ppermute | solution.py:345
  38.7 0.0 collective-permute-start.2
  38.7 7.1 %collective-permute-done.2.refs_3_.refs_19_ = bf16[128,1152]{1,0:T(8,128)(2,1)S(1)} collective-permute-done((bf16[128,1152]{1,0:T(8,128)(2,1)S(1)}, bf16[128,1152]{1,0:T(8,128)(2,1)S(1)}, u32[]{:S(2)}, u32[]{:S(2)}) %collective-permute-start.2) | collective-permute-done | bytes 294944 | tf_op jit(solution)/shard_map/ppermute | solution.py:345
  45.8 0.0 collective-permute-start.6
  45.8 0.0 collective-permute-done.3.refs_5_
  45.8 0.5 collective-permute-start.9
  46.3 0.0 collective-permute-done.4.refs_6_
  46.3 0.1 collective-permute-start.5
  46.4 2.5 %collective-permute-done.7.refs_10_ = bf16[1024,384]{1,0:T(8,128)(2,1)S(1)} collective-permute-done((bf16[1024,384]{1,0:T(8,128)(2,1)}, bf16[1024,384]{1,0:T(8,128)(2,1)S(1)}, u32[]{:S(2)}, u32[]{:S(2)}) %collective-permute-start.7) | collective-permute-done | bytes 786464 | tf_op jit(solution)/shard_map/ppermute | solution.py:345
  48.9 0.0 collective-permute-start.8
  48.9 16.4 %collective-permute-done.10.refs_14_ = bf16[384,1024]{1,0:T(8,128)(2,1)S(1)} collective-permute-done((bf16[384,1024]{1,0:T(8,128)(2,1)}, bf16[384,1024]{1,0:T(8,128)(2,1)S(1)}, u32[]{:S(2)}, u32[]{:S(2)}) %collective-permute-start.10) | collective-permute-done | bytes 786464 | tf_op jit(solution)/shard_map/ppermute | solution.py:345
  65.3 0.1 collective-permute-start.11
  65.3 0.8 pad_add_fusion.which_ref
  66.1 0.0 collective-permute-done.6.refs_9_
  66.1 0.5 collective-permute-start.14
  66.5 0.0 collective-permute-done.9.refs_13_
  66.5 1.6 %collective-permute-start.16 = (bf16[128,1024]{1,0:T(8,128)(2,1)}, bf16[128,1024]{1,0:T(8,128)(2,1)}, u32[]{:S(2)}, u32[]{:S(2)}) collective-permute-start(bf16[128,1024]{1,0:T(8,128)(2,1)} %copy-done.12), channel_id=1, source_target_pairs={{0,4},{1,5},{2,6},{3,7},{4,0},{5,1},{6,2},{7,3},{8,12},{9,13},{10,... | collective-permute-start | bytes 786440 | tf_op jit(solution)/shard_map/ppermute | solution.py:345
  68.2 11.0 %forward.1 = (f32[2,128,1024]{2,1,0:T(8,128)}, bf16[2,128,1024]{2,1,0:T(8,128)(2,1)}, bf16[512,1536]{1,0:T(8,128)(2,1)}, bf16[512,1536]{1,0:T(8,128)(2,1)}, bf16[512,1536]{1,0:T(8,128)(2,1)}) custom-call(s32[4]{0:T(128)} %pad_add_fusion.which_ref, bf16[128,1152]{1,0:T(8,128)(2,1)} %get-tuple-element.14.refs_0_.refs_16_, bf16[128,1152]{1,0:T(8,128)(2,1)} %copy-done.9, ...), custom_call_target="tpu_custom_call" | custom-call | flops 4831838208 | bytes 14155776 | tf_op jit(solution)/shard_map/forward/pallas_call | solution.py:381
  79.2 1.4 collective-permute-done.16.refs_3_
  80.6 12.4 %backward.1 = (f32[2,128,1152]{2,1,0:T(8,128)}, bf16[2,128,1152]{2,1,0:T(8,128)(2,1)}) custom-call(s32[4]{0:T(128)} %pad_add_fusion.which_ref, bf16[128,1024]{1,0:T(8,128)(2,1)} %get-tuple-element.17.refs_0_, bf16[128,1024]{1,0:T(8,128)(2,1)} %collective-permute-done.14.refs_1_, bf16[128,1024]{1,0:T(8,128)(2,1)} %copy-done.12, ...), custom_call_target="tpu_custom_call" | custom-call | flops 4831838208 | bytes 14155776 | tf_op jit(solution)/shard_map/backward/pallas_call | solution.py:415
  93.0 0.5 collective-permute-start.17
  93.5 1.6 %collective-permute-start.12 = (bf16[2,128,1024]{2,1,0:T(8,128)(2,1)S(1)}, bf16[2,128,1024]{2,1,0:T(8,128)(2,1)S(1)}, u32[]{:S(2)}, u32[]{:S(2)}) collective-permute-start(bf16[2,128,1024]{2,1,0:T(8,128)(2,1)S(1)} %copy-done.8), channel_id=1, source_target_pairs={{0,4},{1,5},{2,6},{3,7},{4,0},{5,1},{6,2},{7,3},{8,12},{9,13},{10,... | collective-permute-start | bytes 1572872 | tf_op jit(solution)/shard_map/ppermute | solution.py:345
  95.1 14.4 %collective-permute-done.17.got_ref.near_ref = bf16[2,128,1152]{2,1,0:T(8,128)(2,1)S(1)} collective-permute-done((bf16[2,128,1152]{2,1,0:T(8,128)(2,1)}, bf16[2,128,1152]{2,1,0:T(8,128)(2,1)S(1)}, u32[]{:S(2)}, u32[]{:S(2)}) %collective-permute-start.17) | collective-permute-done | bytes 589856 | tf_op jit(solution)/shard_map/ppermute | solution.py:345
  109.4 0.8 copy-done
  110.2 1.9 %merge_grad.1 = bf16[128,1152]{1,0:T(8,128)(2,1)} custom-call(f32[2,128,1152]{2,1,0:T(8,128)} %get-tuple-element.21.keep_ref, bf16[2,128,1152]{2,1,0:T(8,128)(2,1)} %copy-done), custom_call_target="tpu_custom_call" | custom-call | tf_op jit(solution)/shard_map/merge_grad/pallas_call | solution.py:401
  112.1 0.3 collective-permute-start.18
  112.5 12.1 %collective-permute-done.12.got_ref.near_ref = bf16[2,128,1024]{2,1,0:T(8,128)(2,1)S(1)} collective-permute-done((bf16[2,128,1024]{2,1,0:T(8,128)(2,1)S(1)}, bf16[2,128,1024]{2,1,0:T(8,128)(2,1)S(1)}, u32[]{:S(2)}, u32[]{:S(2)}) %collective-permute-start.12) | collective-permute-done | bytes 524320 | tf_op jit(solution)/shard_map/ppermute | solution.py:345
  124.6 0.8 copy-done.1
  125.4 1.9 %merge_mixed.1 = bf16[128,1024]{1,0:T(8,128)(2,1)} custom-call(f32[2,128,1024]{2,1,0:T(8,128)} %get-tuple-element.15.keep_ref, bf16[2,128,1024]{2,1,0:T(8,128)(2,1)} %copy-done.1), custom_call_target="tpu_custom_call" | custom-call | tf_op jit(solution)/shard_map/merge_mixed/pallas_call | solution.py:401
  127.3 0.0 collective-permute-start.13
  127.3 12.5 %collective-permute-done.13.far_ref = bf16[128,1024]{1,0:T(8,128)(2,1)S(1)} collective-permute-done((bf16[128,1024]{1,0:T(8,128)(2,1)}, bf16[128,1024]{1,0:T(8,128)(2,1)S(1)}, u32[]{:S(2)}, u32[]{:S(2)}) %collective-permute-start.13) | collective-permute-done | bytes 262176 | tf_op jit(solution)/shard_map/ppermute | solution.py:345
  139.8 0.7 copy-done.3
  140.5 2.0 %finish_mixed.1 = bf16[128,1024]{1,0:T(8,128)(2,1)} custom-call(f32[2,128,1024]{2,1,0:T(8,128)} %get-tuple-element.15.keep_ref, bf16[2,128,1024]{2,1,0:T(8,128)(2,1)} %copy-done.1, bf16[128,1024]{1,0:T(8,128)(2,1)} %copy-done.3), custom_call_target="tpu_custom_call" | custom-call | tf_op jit(solution)/shard_map/finish_mixed/pallas_call | solution.py:438
  142.5 0.7 copy-done.2
  143.2 2.8 %finish_grad.1 = (bf16[128,1024]{1,0:T(8,128)(2,1)}, f32[128,8]{1,0:T(8,128)}) custom-call(f32[2,128,1152]{2,1,0:T(8,128)} %get-tuple-element.21.keep_ref, bf16[2,128,1152]{2,1,0:T(8,128)(2,1)} %copy-done, bf16[128,1152]{1,0:T(8,128)(2,1)} %copy-done.2, s32[128,8]{1,0:T(8,128)} %copy.11.ids_ref), custom_call_target="tpu_custom_call" | custom-call | tf_op jit(solution)/shard_map/finish_grad/pallas_call | solution.py:447
  146.0 1.5 %copy.14 = f32[128,8]{0,1:T(8,128)} copy(f32[128,8]{1,0:T(8,128)} %get-tuple-element.27) | data formatting | bytes 8192
  (27 shorter events, 0.1 us)
Async XLA Ops:
  5.7 16.3 %collective-permute-start.15 = (bf16[128,1024]{1,0:T(8,128)(2,1)}, bf16[128,1024]{1,0:T(8,128)(2,1)S(1)}, u32[]{:S(2)}, u32[]{:S(2)}) collective-permute-start(bf16[128,1024]{1,0:T(8,128)(2,1)} %get-tuple-element.17.refs_0_), channel_id=1, source_target_pairs={{0,8},{1,9},{2,10},{3,11},{4,12},{5,13},{6,14},{7,15},{8,0},{9,1},... | collective-permute-start | bytes 786440 | tf_op jit(solution)/shard_map/ppermute | solution.py:345
  9.8 13.8 %collective-permute-start = (bf16[128,1152]{1,0:T(8,128)(2,1)}, bf16[128,1152]{1,0:T(8,128)(2,1)S(1)}, u32[]{:S(2)}, u32[]{:S(2)}) collective-permute-start(bf16[128,1152]{1,0:T(8,128)(2,1)} %get-tuple-element.14.refs_0_.refs_16_), channel_id=1, source_target_pairs={{0,4},{1,5},{2,6},{3,7},{4,0},{5,1},{6,2},{7,3},{8,12},{9,13},{10,... | collective-permute-start | bytes 884744 | tf_op jit(solution)/shard_map/ppermute | solution.py:345
  11.4 34.4 %collective-permute-start.3 = (bf16[1024,384]{1,0:T(8,128)(2,1)}, bf16[1024,384]{1,0:T(8,128)(2,1)S(1)}, u32[]{:S(2)}, u32[]{:S(2)}) collective-permute-start(bf16[1024,384]{1,0:T(8,128)(2,1)} %bitcast.8), channel_id=1, source_target_pairs={{0,1},{1,0},{2,3},{3,2},{4,5},{5,4},{6,7},{7,6},{8,9},{9,8},{10,11... | collective-permute-start | bytes 2359304 | tf_op jit(solution)/shard_map/ppermute | solution.py:345
  11.4 34.9 %collective-permute-start.4 = (bf16[1024,384]{1,0:T(8,128)(2,1)}, bf16[1024,384]{1,0:T(8,128)(2,1)S(1)}, u32[]{:S(2)}, u32[]{:S(2)}) collective-permute-start(bf16[1024,384]{1,0:T(8,128)(2,1)} %bitcast.9), channel_id=1, source_target_pairs={{0,2},{1,3},{2,0},{3,1},{4,6},{5,7},{6,4},{7,5},{8,10},{9,11},{10,... | collective-permute-start | bytes 2359304 | tf_op jit(solution)/shard_map/ppermute | solution.py:345
  12.9 36.0 %collective-permute-start.7 = (bf16[1024,384]{1,0:T(8,128)(2,1)}, bf16[1024,384]{1,0:T(8,128)(2,1)S(1)}, u32[]{:S(2)}, u32[]{:S(2)}) collective-permute-start(bf16[1024,384]{1,0:T(8,128)(2,1)} %bitcast.12), channel_id=1, source_target_pairs={{0,2},{1,3},{2,0},{3,1},{4,6},{5,7},{6,4},{7,5},{8,10},{9,11},{10,... | collective-permute-start | bytes 2359304 | tf_op jit(solution)/shard_map/ppermute | solution.py:345
  22.0 1.5 %copy-start.12 = (bf16[128,1024]{1,0:T(8,128)(2,1)}, bf16[128,1024]{1,0:T(8,128)(2,1)S(1)}, u32[]{:S(2)}) copy-start(bf16[128,1024]{1,0:T(8,128)(2,1)S(1)} %collective-permute-done.15.refs_2_) | copy-start | bytes 786436
  22.0 43.2 %collective-permute-start.10 = (bf16[384,1024]{1,0:T(8,128)(2,1)}, bf16[384,1024]{1,0:T(8,128)(2,1)S(1)}, u32[]{:S(2)}, u32[]{:S(2)}) collective-permute-start(bf16[384,1024]{1,0:T(8,128)(2,1)} %bitcast.16), channel_id=1, source_target_pairs={{0,2},{1,3},{2,0},{3,1},{4,6},{5,7},{6,4},{7,5},{8,10},{9,11},{10,... | collective-permute-start | bytes 2359304 | tf_op jit(solution)/shard_map/ppermute | solution.py:345
  23.6 44.6 %copy-start.9 = (bf16[128,1152]{1,0:T(8,128)(2,1)}, bf16[128,1152]{1,0:T(8,128)(2,1)S(1)}, u32[]{:S(2)}) copy-start(bf16[128,1152]{1,0:T(8,128)(2,1)S(1)} %collective-permute-done.refs_1_.refs_17_) | copy-start | bytes 884740
  23.6 15.1 %collective-permute-start.1 = (bf16[128,1152]{1,0:T(8,128)(2,1)}, bf16[128,1152]{1,0:T(8,128)(2,1)S(1)}, u32[]{:S(2)}, u32[]{:S(2)}) collective-permute-start(bf16[128,1152]{1,0:T(8,128)(2,1)} %get-tuple-element.14.refs_0_.refs_16_), channel_id=1, source_target_pairs={{0,8},{1,9},{2,10},{3,11},{4,12},{5,13},{6,14},{7,15},{8,0},{9,1},... | collective-permute-start | bytes 884744 | tf_op jit(solution)/shard_map/ppermute | solution.py:345
  38.7 26.6 %copy-start.10 = (bf16[128,1152]{1,0:T(8,128)(2,1)}, bf16[128,1152]{1,0:T(8,128)(2,1)S(1)}, u32[]{:S(2)}) copy-start(bf16[128,1152]{1,0:T(8,128)(2,1)S(1)} %collective-permute-done.1.refs_2_.refs_18_) | copy-start | bytes 884740
  38.7 7.1 %collective-permute-start.2 = (bf16[128,1152]{1,0:T(8,128)(2,1)S(1)}, bf16[128,1152]{1,0:T(8,128)(2,1)S(1)}, u32[]{:S(2)}, u32[]{:S(2)}) collective-permute-start(bf16[128,1152]{1,0:T(8,128)(2,1)S(1)} %collective-permute-done.1.refs_2_.refs_18_), channel_id=1, source_target_pairs={{0,4},{1,5},{2,6},{3,7},{4,0},{5,1},{6,2},{7,3},{8,12},{9,13},{10,... | collective-permute-start | bytes 884744 | tf_op jit(solution)/shard_map/ppermute | solution.py:345
  45.8 19.5 %copy-start.11 = (bf16[128,1152]{1,0:T(8,128)(2,1)}, bf16[128,1152]{1,0:T(8,128)(2,1)S(1)}, u32[]{:S(2)}) copy-start(bf16[128,1152]{1,0:T(8,128)(2,1)S(1)} %collective-permute-done.2.refs_3_.refs_19_) | copy-start | bytes 884740
  45.8 20.3 %collective-permute-start.6 = (bf16[1024,384]{1,0:T(8,128)(2,1)}, bf16[1024,384]{1,0:T(8,128)(2,1)}, u32[]{:S(2)}, u32[]{:S(2)}) collective-permute-start(bf16[1024,384]{1,0:T(8,128)(2,1)} %bitcast.13), channel_id=1, source_target_pairs={{0,1},{1,0},{2,3},{3,2},{4,5},{5,4},{6,7},{7,6},{8,9},{9,8},{10,11... | collective-permute-start | bytes 2359304 | tf_op jit(solution)/shard_map/ppermute | solution.py:345
  45.8 22.4 %copy-start.4 = (bf16[1024,384]{1,0:T(8,128)(2,1)}, bf16[1024,384]{1,0:T(8,128)(2,1)S(1)}, u32[]{:S(2)}) copy-start(bf16[1024,384]{1,0:T(8,128)(2,1)S(1)} %collective-permute-done.3.refs_5_) | copy-start | bytes 2359300
  45.8 20.8 %collective-permute-start.9 = (bf16[384,1024]{1,0:T(8,128)(2,1)}, bf16[384,1024]{1,0:T(8,128)(2,1)}, u32[]{:S(2)}, u32[]{:S(2)}) collective-permute-start(bf16[384,1024]{1,0:T(8,128)(2,1)} %bitcast.17), channel_id=1, source_target_pairs={{0,1},{1,0},{2,3},{3,2},{4,5},{5,4},{6,7},{7,6},{8,9},{9,8},{10,11... | collective-permute-start | bytes 2359304 | tf_op jit(solution)/shard_map/ppermute | solution.py:345
  46.3 21.9 %copy-start.5 = (bf16[1024,384]{1,0:T(8,128)(2,1)}, bf16[1024,384]{1,0:T(8,128)(2,1)S(1)}, u32[]{:S(2)}) copy-start(bf16[1024,384]{1,0:T(8,128)(2,1)S(1)} %collective-permute-done.4.refs_6_) | copy-start | bytes 2359300
  46.3 21.8 %collective-permute-start.5 = (bf16[1024,384]{1,0:T(8,128)(2,1)S(1)}, bf16[1024,384]{1,0:T(8,128)(2,1)}, u32[]{:S(2)}, u32[]{:S(2)}) collective-permute-start(bf16[1024,384]{1,0:T(8,128)(2,1)S(1)} %collective-permute-done.4.refs_6_), channel_id=1, source_target_pairs={{0,1},{1,0},{2,3},{3,2},{4,5},{5,4},{6,7},{7,6},{8,9},{9,8},{10,11... | collective-permute-start | bytes 2359304 | tf_op jit(solution)/shard_map/ppermute | solution.py:345
  48.9 19.3 %copy-start.6 = (bf16[1024,384]{1,0:T(8,128)(2,1)}, bf16[1024,384]{1,0:T(8,128)(2,1)S(1)}, u32[]{:S(2)}) copy-start(bf16[1024,384]{1,0:T(8,128)(2,1)S(1)} %collective-permute-done.7.refs_10_) | copy-start | bytes 2359300
  48.9 19.3 %collective-permute-start.8 = (bf16[1024,384]{1,0:T(8,128)(2,1)S(1)}, bf16[1024,384]{1,0:T(8,128)(2,1)}, u32[]{:S(2)}, u32[]{:S(2)}) collective-permute-start(bf16[1024,384]{1,0:T(8,128)(2,1)S(1)} %collective-permute-done.7.refs_10_), channel_id=1, source_target_pairs={{0,1},{1,0},{2,3},{3,2},{4,5},{5,4},{6,7},{7,6},{8,9},{9,8},{10,11... | collective-permute-start | bytes 2359304 | tf_op jit(solution)/shard_map/ppermute | solution.py:345
  65.3 2.9 %copy-start.7 = (bf16[384,1024]{1,0:T(8,128)(2,1)}, bf16[384,1024]{1,0:T(8,128)(2,1)S(1)}, u32[]{:S(2)}) copy-start(bf16[384,1024]{1,0:T(8,128)(2,1)S(1)} %collective-permute-done.10.refs_14_) | copy-start | bytes 2359300
  65.3 2.9 %collective-permute-start.11 = (bf16[384,1024]{1,0:T(8,128)(2,1)S(1)}, bf16[384,1024]{1,0:T(8,128)(2,1)}, u32[]{:S(2)}, u32[]{:S(2)}) collective-permute-start(bf16[384,1024]{1,0:T(8,128)(2,1)S(1)} %collective-permute-done.10.refs_14_), channel_id=1, source_target_pairs={{0,1},{1,0},{2,3},{3,2},{4,5},{5,4},{6,7},{7,6},{8,9},{9,8},{10,11... | collective-permute-start | bytes 2359304 | tf_op jit(solution)/shard_map/ppermute | solution.py:345
  66.1 13.1 %collective-permute-start.14 = (bf16[128,1024]{1,0:T(8,128)(2,1)}, bf16[128,1024]{1,0:T(8,128)(2,1)}, u32[]{:S(2)}, u32[]{:S(2)}) collective-permute-start(bf16[128,1024]{1,0:T(8,128)(2,1)} %get-tuple-element.17.refs_0_), channel_id=1, source_target_pairs={{0,4},{1,5},{2,6},{3,7},{4,0},{5,1},{6,2},{7,3},{8,12},{9,13},{10,... | collective-permute-start | bytes 786440 | tf_op jit(solution)/shard_map/ppermute | solution.py:345
  66.5 14.0 %collective-permute-start.16 = (bf16[128,1024]{1,0:T(8,128)(2,1)}, bf16[128,1024]{1,0:T(8,128)(2,1)}, u32[]{:S(2)}, u32[]{:S(2)}) collective-permute-start(bf16[128,1024]{1,0:T(8,128)(2,1)} %copy-done.12), channel_id=1, source_target_pairs={{0,4},{1,5},{2,6},{3,7},{4,0},{5,1},{6,2},{7,3},{8,12},{9,13},{10,... | collective-permute-start | bytes 786440 | tf_op jit(solution)/shard_map/ppermute | solution.py:345
  80.6 12.9 %copy-start.8 = (bf16[2,128,1024]{2,1,0:T(8,128)(2,1)S(1)}, bf16[2,128,1024]{2,1,0:T(8,128)(2,1)}, u32[]{:S(2)}) copy-start(bf16[2,128,1024]{2,1,0:T(8,128)(2,1)} %get-tuple-element.16) | copy-start | bytes 1572868
  93.0 16.5 %collective-permute-start.17 = (bf16[2,128,1152]{2,1,0:T(8,128)(2,1)}, bf16[2,128,1152]{2,1,0:T(8,128)(2,1)S(1)}, u32[]{:S(2)}, u32[]{:S(2)}) collective-permute-start(bf16[2,128,1152]{2,1,0:T(8,128)(2,1)} %get-tuple-element.22), channel_id=1, source_target_pairs={{0,4},{1,5},{2,6},{3,7},{4,0},{5,1},{6,2},{7,3},{8,12},{9,13},{10,... | collective-permute-start | bytes 1769480 | tf_op jit(solution)/shard_map/ppermute | solution.py:345
  93.5 31.1 %collective-permute-start.12 = (bf16[2,128,1024]{2,1,0:T(8,128)(2,1)S(1)}, bf16[2,128,1024]{2,1,0:T(8,128)(2,1)S(1)}, u32[]{:S(2)}, u32[]{:S(2)}) collective-permute-start(bf16[2,128,1024]{2,1,0:T(8,128)(2,1)S(1)} %copy-done.8), channel_id=1, source_target_pairs={{0,4},{1,5},{2,6},{3,7},{4,0},{5,1},{6,2},{7,3},{8,12},{9,13},{10,... | collective-permute-start | bytes 1572872 | tf_op jit(solution)/shard_map/ppermute | solution.py:345
  109.4 0.8 copy-start
  112.1 30.3 %collective-permute-start.18 = (bf16[128,1152]{1,0:T(8,128)(2,1)}, bf16[128,1152]{1,0:T(8,128)(2,1)S(1)}, u32[]{:S(2)}, u32[]{:S(2)}) collective-permute-start(bf16[128,1152]{1,0:T(8,128)(2,1)} %merge_grad.1), channel_id=1, source_target_pairs={{0,8},{1,9},{2,10},{3,11},{4,12},{5,13},{6,14},{7,15},{8,0},{9,1},... | collective-permute-start | bytes 884744 | tf_op jit(solution)/shard_map/ppermute | solution.py:345
  124.6 0.8 copy-start.1
  127.3 12.5 %collective-permute-start.13 = (bf16[128,1024]{1,0:T(8,128)(2,1)}, bf16[128,1024]{1,0:T(8,128)(2,1)S(1)}, u32[]{:S(2)}, u32[]{:S(2)}) collective-permute-start(bf16[128,1024]{1,0:T(8,128)(2,1)} %merge_mixed.1), channel_id=1, source_target_pairs={{0,8},{1,9},{2,10},{3,11},{4,12},{5,13},{6,14},{7,15},{8,0},{9,1},... | collective-permute-start | bytes 786440 | tf_op jit(solution)/shard_map/ppermute | solution.py:345
  139.8 0.7 copy-start.3
  142.5 0.7 copy-start.2
